TPU v7x, 32 devices: a whole 2x2x4 slice. The times are simulated.
32 devices in a mesh: row: 2 (over x), col: 16 (over z, y, core).
Axes of the slice: x: 2, y: 2, z: 4, core: 2. Of those that a mesh axis runs over, the one named last changes fastest.
Arguments:
- activations: bfloat16 [128, 8192], P('col', 'row'), may hold values from -6 to 6
- up_weight: bfloat16 [8192, 53248], P('row', 'col'), may hold values from -0.0625 to 0.0625
- out_grad: bfloat16 [128, 53248], P('row', 'col'), may hold values from -6 to 6
- round_seed: int32 [1], replicated, may hold values from 0 to 1073741823
- counter_base: int32 [128], P('row'), may hold values from 0 to 1073741823
Outputs:
- weight_grad: float32 [8192, 53248], P('row', 'col')
- input_grad: bfloat16 [128, 8192], P('col', 'row')
All inputs are finite; a program needn't handle non-finite values.
Results may differ from a plain program's by a relative error of at most 0.015.
Values may be sent and summed in bfloat16 or wider, within the bound.
No kernel may reach another device: no remote copies, remote signals or barrier semaphores. Data moves between devices by JAX's collectives and lax.ppermute only.
A program may use at most 192 MiB of HBM per device.

v0:
```python
import jax
import jax.numpy as jnp
from jax import lax
from jax.sharding import PartitionSpec as P


def stochastic_round(grad, counter_base, round_seed, col_first):
    columns = col_first + lax.broadcasted_iota(jnp.int32, grad.shape, 1)
    counter = counter_base[:, None] + columns
    mixed = counter * jnp.int32(747796405) + round_seed[0] * jnp.int32(1013904223)
    mixed = mixed ^ mixed >> 15
    mixed = mixed * jnp.int32(277803737)
    mixed = mixed ^ mixed >> 16
    level = (mixed & 255).astype(jnp.float32)
    scaled = grad.astype(jnp.float32) * 4.0 + (level + 0.5) / 256.0
    return (jnp.floor(scaled) / 4.0).astype(jnp.bfloat16)


def contract(left, right):
    return lax.dot_general(
        left, right, (((0,), (0,)), ((), ())), preferred_element_type=jnp.float32
    )


def project(grad_rows, weight):
    return lax.dot_general(
        grad_rows, weight, (((1,), (1,)), ((), ())), preferred_element_type=jnp.float32
    )


def fold_panels(activations, combine, initial):
    everyone = lax.all_gather(activations, "col", axis=0, tiled=True)
    return combine(initial, everyone, 0)


def shards(activations, up_weight, out_grad, round_seed, counter_base):
    ff_local = out_grad.shape[1]
    d_local = activations.shape[1]
    col_first = lax.axis_index("col") * ff_local
    quantized = stochastic_round(out_grad, counter_base, round_seed, col_first)
    total_tokens = activations.shape[0] * lax.axis_size("col")
    scaling = total_tokens ** (-0.5)
    grad_zero = jnp.zeros((d_local, ff_local), jnp.float32)
    everything = lax.all_gather(quantized, "row", axis=0, tiled=True)

    def accumulate(total, panel, offset):
        return contract(panel, everything)

    weight_grad = fold_panels(activations, accumulate, grad_zero)
    input_grad = lax.psum_scatter(
        project(everything, up_weight).astype(jnp.bfloat16), "col", scatter_dimension=0, tiled=True
    )
    return (weight_grad * scaling, input_grad)


def solution(mesh):
    placed = (P("col", "row"), P("row", "col"), P("row", "col"), P(), P("row"))
    return jax.shard_map(
        shards,
        mesh=mesh,
        in_specs=placed,
        out_specs=(P("row", "col"), P("col", "row")),
        check_vma=False,
    )
```

profile of v0, /device:TPU:0, one launch (start us, length us, event | category | flops | bytes accessed | tf_op | source)
XLA Modules:
  0.0 130.5 jit_solution(6275972824914543225)
XLA Ops:
  7.2 0.0 all-gather.2.cloned.1.call-start
  7.2 0.7 all-gather.2.cloned.1.call-update
  7.9 0.0 reduce-scatter.2.cloned.1.call-start
  8.6 1.6 %fusion.8 = bf16[64,3328]{1,0:T(8,128)(2,1)S(1)} fusion(bf16[64,3328]{1,0:T(8,128)(2,1)} %param.7, s32[]{:T(128)} %bitcast, s32[3328]{0:T(1024)S(1)} %iota_add_fusion, s32[64]{0:T(128)} %param.9), kind=kLoop, calls=%fused_computation.12 | loop fusion | flops 3833856 | bytes 865540 | tf_op jit(solution)/shard_map/convert_element_type | solution.py:16
  10.2 13.5 %all_gather.6 = bf16[128,3328]{1,0:T(8,128)(2,1)S(1)} all-gather(bf16[64,3328]{1,0:T(8,128)(2,1)S(1)} %fusion.8), channel_id=1, replica_groups=mesh['row'=2,'col'=16] {'row'}, dimensions={0}, use_global_device_ids=true | all-gather | bytes 1277952 | tf_op jit(solution)/shard_map/all_gather | solution.py:44
  23.6 15.0 %convolution_convert_fusion = bf16[128,4096]{1,0:T(8,128)(2,1)} fusion(bf16[128,3328]{1,0:T(8,128)(2,1)S(1)} %all_gather.6, bf16[4096,3328]{1,0:T(8,128)(2,1)} %param.6), kind=kOutput, calls=%fused_computation.1 | convolution fusion | flops 3490185216 | bytes 29163520 | tf_op jit(solution)/shard_map/dot_general | solution.py:26
  38.6 0.0 reduce-scatter.2.cloned.1.call-update
  38.7 12.1 %all-gather.2.cloned.1.call-done = bf16[128,4096]{1,0:T(8,128)(2,1)} async-done(((bf16[8,4096]{1,0:T(8,128)(2,1)}), bf16[128,4096]{1,0:T(8,128)(2,1)}) %all-gather.2.cloned.1.call-update) | async-done | bytes 1048592 | tf_op jit(solution)/shard_map/all_gather | solution.py:32
  50.8 22.8 %multiply_bitcast_fusion = f32[4096,3328]{0,1:T(8,128)} fusion(bf16[128,3328]{1,0:T(8,128)(2,1)S(1)} %all_gather.6, bf16[128,4096]{1,0:T(8,128)(2,1)} %all-gather.2.cloned.1.call-done), kind=kOutput, calls=%fused_computation | convolution fusion | flops 3503292416 | bytes 56426496 | tf_op jit(solution)/shard_map/dot_general | solution.py:20
  73.6 50.1 %copy.7 = f32[4096,3328]{1,0:T(8,128)} copy(f32[4096,3328]{0,1:T(8,128)} %multiply_bitcast_fusion) | data formatting | bytes 109051904
  123.7 0.0 reduce-scatter.2.cloned.1.call-done
  (1 shorter events, 0.0 us)
Async XLA Ops:
  7.2 43.6 %all-gather.2.cloned.1.call-start = ((), (), s32[]{:S(2)}) async-start(), calls=%async_computation.1 | async-start | bytes 1114112 | tf_op jit(solution)/shard_map/all_gather | solution.py:32
  7.9 115.8 %reduce-scatter.2.cloned.1.call-start = ((), (), s32[]{:S(2)}) async-start(), calls=%async_computation.2 | async-start | bytes 1114112 | tf_op jit(solution)/shard_map/reduce_scatter | solution.py:50
Sparse Core Ops, SparseCore 0:
  10.1 40.5 all-gather.1
  54.9 56.5 reduce-scatter.1
where the time goes:
time: 131 us
  local copies, waits for them, and re-layouts  50.1 us (38%)
  matrix products  37.8 us (29%)
  between operations  14.7 us (11%)
  blocking collectives  13.5 us (10%)
  waiting for transfers between devices  12.8 us (10%)
  other arithmetic  1.56 us (1%)
    unnamed x1, local copies, waits for them, and re-layouts  50.1 us
    dot_general x1, matrix products, contract(): lax.dot_general(left, right, (((0,), (0,)), ((), ())), preferred_element_...  22.8 us
    dot_general x1, matrix products, project(): lax.dot_general(grad_rows, weight, (((1,), (1,)), ((), ())), preferred_el...  15 us
    all_gather x1, blocking collectives, shards(): everything = lax.all_gather(quantized, 'row', axis=0, tiled=True)  13.5 us
    all_gather x1, waiting for transfers between devices, fold_panels(): everyone = lax.all_gather(activations, 'col', axis=0, tiled=True)  12.1 us
  transfers between devices with their start and end apart: 2, of which 1 were waited for; matrix products, arithmetic and copies ran while one was open for 69% of the time, Pallas kernels for 0%

commit v1 on v0

--- a/solution.py
+++ b/solution.py
@@ -29,7 +29,10 @@
 
 
 def fold_panels(activations, combine, initial):
-    everyone = lax.all_gather(activations, "col", axis=0, tiled=True)
+    size = lax.axis_size("col")
+    blocks = jnp.stack([activations for _ in range(size)])
+    blocks = lax.all_to_all(blocks, "col", split_axis=0, concat_axis=0)
+    everyone = jnp.concatenate(blocks, axis=0)
     return combine(initial, everyone, 0)
 
 

time: 131 us -> 126 us (0.962)
  waiting for transfers between devices: 12.8 us -> 0.02 us
  starting transfers between devices: 0.08 us -> 7.46 us
  local copies, waits for them, and re-layouts: 50.1 us -> 52 us
    all_gather x1 -> x0, waiting for transfers between devices: 12.1 us -> none  [fold_panels(): everyone = lax.all_gather(activations, 'col', axis=0, tiled=True)]
    all_to_all x0 -> x1, starting transfers between devices: none -> 7.41 us  [fold_panels(): blocks = lax.all_to_all(blocks, 'col', split_axis=0, concat_axis=0)]
    another operation x0 -> x1, local copies, waits for them, and re-layouts: none -> 1.91 us  [fold_panels(): blocks = jnp.stack([activations for _ in range(size)])]
  transfers between devices with their start and end apart: 2 -> 2, of which waited for: 1 -> 0; matrix products, arithmetic and copies ran while one was open for 69% -> 71% of each run, Pallas kernels for 0% -> 0%
where the time goes in v1:
time: 126 us; the launch traced here: 125 us
  local copies, waits for them, and re-layouts  52 us (41%)
  matrix products  36.6 us (29%)
  between operations  14.7 us (12%)
  blocking collectives  12.8 us (10%)
  starting transfers between devices  7.46 us (6%)
  other arithmetic  1.56 us (1%)
    unnamed x1, local copies, waits for them, and re-layouts  50.1 us
    dot_general x1, matrix products, contract(): lax.dot_general(left, right, (((0,), (0,)), ((), ())), preferred_element_...  21.6 us
    dot_general x1, matrix products, project(): lax.dot_general(grad_rows, weight, (((1,), (1,)), ((), ())), preferred_el...  15 us
    all_gather x1, blocking collectives, shards(): everything = lax.all_gather(quantized, 'row', axis=0, tiled=True)  12.8 us
    all_to_all x1, starting transfers between devices, fold_panels(): blocks = lax.all_to_all(blocks, 'col', split_axis=0, concat_axis=0)  7.41 us
  transfers between devices with their start and end apart: 2, of which 0 were waited for; matrix products, arithmetic and copies ran while one was open for 71% of the time, Pallas kernels for 0%

profile of v1, /device:TPU:0, one launch (start us, length us, event | category | flops | bytes accessed | tf_op | source)
XLA Modules:
  0.0 125.2 jit_solution(5906629094561902594)
XLA Ops:
  7.2 1.9 %stack.2 = bf16[16,8,4096]{2,1,0:T(8,128)(2,1)} broadcast(bf16[8,4096]{1,0:T(8,128)(2,1)} %param.5), dimensions={1,2} | broadcast | bytes 1114112 | tf_op jit(solution)/shard_map/stack | solution.py:33
  9.1 7.4 %all-to-all-start = ((bf16[16,8,4096]{2,1,0:T(8,128)(2,1)}), bf16[16,8,4096]{2,1,0:T(8,128)(2,1)S(1)}, u32[]{:S(2)}, u32[]{:S(2)}) async-start(bf16[16,8,4096]{2,1,0:T(8,128)(2,1)} %stack.2), calls=%async_computation | async-start | bytes 2097152 | tf_op jit(solution)/shard_map/all_to_all | solution.py:34
  16.5 0.0 reduce-scatter.2.cloned.1.call-start
  17.2 1.6 %fusion.9 = bf16[64,3328]{1,0:T(8,128)(2,1)S(1)} fusion(bf16[64,3328]{1,0:T(8,128)(2,1)} %param.7, s32[]{:T(128)} %bitcast, s32[3328]{0:T(1024)S(1)} %iota_add_fusion, s32[64]{0:T(128)} %param.9), kind=kLoop, calls=%fused_computation.13 | loop fusion | flops 3833856 | bytes 865540 | tf_op jit(solution)/shard_map/convert_element_type | solution.py:16
  18.8 12.8 %all_gather.3 = bf16[128,3328]{1,0:T(8,128)(2,1)S(1)} all-gather(bf16[64,3328]{1,0:T(8,128)(2,1)S(1)} %fusion.9), channel_id=1, replica_groups=mesh['row'=2,'col'=16] {'row'}, dimensions={0}, use_global_device_ids=true | all-gather | bytes 1277952 | tf_op jit(solution)/shard_map/all_gather | solution.py:47
  31.6 15.0 %convolution_convert_fusion = bf16[128,4096]{1,0:T(8,128)(2,1)} fusion(bf16[128,3328]{1,0:T(8,128)(2,1)S(1)} %all_gather.3, bf16[4096,3328]{1,0:T(8,128)(2,1)} %param.6), kind=kOutput, calls=%fused_computation.1 | convolution fusion | flops 3490185216 | bytes 29163520 | tf_op jit(solution)/shard_map/dot_general | solution.py:26
  46.6 0.0 reduce-scatter.2.cloned.1.call-update
  46.6 0.0 all-to-all-done
  46.6 21.6 %multiply_bitcast_fusion = f32[4096,3328]{0,1:T(8,128)} fusion(bf16[128,3328]{1,0:T(8,128)(2,1)S(1)} %all_gather.3, bf16[16,8,4096]{2,1,0:T(8,128)(2,1)S(1)} %all-to-all-done), kind=kOutput, calls=%fused_computation | convolution fusion | flops 3503292416 | bytes 56426496 | tf_op jit(solution)/shard_map/dot_general | solution.py:20
  68.2 50.1 %copy.7 = f32[4096,3328]{1,0:T(8,128)} copy(f32[4096,3328]{0,1:T(8,128)} %multiply_bitcast_fusion) | data formatting | bytes 109051904
  118.3 0.0 reduce-scatter.2.cloned.1.call-done
  (1 shorter events, 0.0 us)
Async XLA Ops:
  9.1 37.5 %all-to-all-start = ((bf16[16,8,4096]{2,1,0:T(8,128)(2,1)}), bf16[16,8,4096]{2,1,0:T(8,128)(2,1)S(1)}, u32[]{:S(2)}, u32[]{:S(2)}) async-start(bf16[16,8,4096]{2,1,0:T(8,128)(2,1)} %stack.2), calls=%async_computation | async-start | bytes 2097152 | tf_op jit(solution)/shard_map/all_to_all | solution.py:34
  16.5 101.8 %reduce-scatter.2.cloned.1.call-start = ((), (), s32[]{:S(2)}) async-start(), calls=%async_computation.2 | async-start | bytes 1114112 | tf_op jit(solution)/shard_map/reduce_scatter | solution.py:53
Sparse Core Ops, SparseCore 0:
  46.7 58.5 reduce-scatter.1
